TPU v7x, 32 devices: a whole 2x2x4 slice. The times are simulated.
32 devices in a mesh: groups: 2 (over y), blk: 4 (over z), comp: 2 (over x), lat: 2 (over core).
Axes of the slice: x: 2, y: 2, z: 4, core: 2. Of those that a mesh axis runs over, the one named last changes fastest.
Arguments:
- rhs: float32 [96, 2, 4, 2048], P(('groups', 'comp'), None, 'blk'), parts along dimension 0, may hold values from -6 to 6
- legendre: bfloat16 [4, 2048, 32], P('blk', None, 'lat'), may hold values from -0.03125 to 0.03125
- beam: float32 [24, 2048], replicated, may hold values from 0.3 to 1
- mixing: float32 [24, 48], P(None, 'comp'), may hold values from -0.875 to 0.875
- prior: float32 [48, 2048], P('comp'), may hold values from 0.5 to 4
- inv_noise: float32 [24, 32, 4096], P('comp', ('blk', 'lat')), may hold values from 0.25 to 4
- mask_flags: int32 [24, 32], P('comp', ('blk', 'lat')), may hold values 0 or 1
- cycle_len: int32 [32], P('lat'), may hold values from 16 to 4096, as said below
- cycle_slot: int32 [32], P('lat'), may hold values from 0 to 15, as said below
- m_values: int32 [4], replicated, may hold values from 0 to 2047, as said below
Outputs:
- solution: float32 [96, 2, 4, 2048], P(('groups', 'comp'), None, 'blk'), parts along dimension 0
- residual: float32 [96, 2, 4, 2048], P(('groups', 'comp'), None, 'blk'), parts along dimension 0
There are 2 independent parts, one for each index of `groups`. A program takes and returns all parts, laid end to end along the dimension named above; an argument that names none is the same for every part. Nothing has to cross between parts.
Inputs may be any that keep to these rules, and one draw needn't show every extreme that they name: `cycle_len`: lengths are multiples of 4; each band (aligned block of 16 entries) holds a cycle of exactly 4096 pixels. `cycle_slot`: each aligned block of 16 entries is a permutation of 0 to 15. `m_values`: the m values are distinct, and both 0 and 2047 occur.
All inputs are finite; a program needn't handle non-finite values. No bound on the sum of `mask_flags` on one device may be relied on, other than what follows from the above.
Results may differ from a plain program's by a relative error of at most 0.023.
Values may be sent and summed in bfloat16 or wider, within the bound.
A program may use at most 64 MiB of HBM per device.

v0:
```python
import math
import jax
import jax.numpy as jnp
from jax import lax
from jax.sharding import PartitionSpec as P

ITERS = 3
HIGHEST_PRECISION = lax.Precision.HIGHEST


def cycle_table(m_values, length, pixel_count):
    pixels = jnp.arange(pixel_count, dtype=jnp.int32)
    phase_ids = m_values[:, None] * (2 * pixels[None, :] + 1) % (2 * length)
    angles = math.pi * phase_ids.astype(jnp.float32) / length.astype(jnp.float32)
    inside = (pixels < length)[None, :]
    cosine = jnp.where(inside, jnp.cos(angles), jnp.float32(0.0))
    sine_part = jnp.where(inside, -jnp.sin(angles), jnp.float32(0.0))
    return jnp.stack([cosine, sine_part]).astype(jnp.bfloat16)


def local(
    rhs, legendre, beam, mixing, prior, inv_noise, mask_flags, cycle_len, cycle_slot, m_values
):
    cycle_count = inv_noise.shape[1]
    pixel_count = inv_noise.shape[2]
    channel_width = inv_noise.shape[0]
    owner_index = lax.axis_index("blk")
    comp_index = lax.axis_index("comp")
    local_ids = lax.dynamic_slice_in_dim(cycle_slot, owner_index * cycle_count, cycle_count)
    local_lengths = cycle_len[local_ids]
    legendre_slot = legendre[:, :, cycle_slot]
    weights = mask_flags.astype(jnp.float32)
    own_beam = lax.dynamic_slice_in_dim(beam, comp_index * channel_width, channel_width, 0)
    stored = jax.vmap(cycle_table, in_axes=(None, 0, None))(m_values, local_lengths, pixel_count)
    solution = jnp.zeros_like(rhs)
    residual = rhs
    direction = rhs
    for iteration in range(ITERS):
        local_mix = jnp.einsum("fc,ckml->fkml", mixing, direction, precision=HIGHEST_PRECISION)
        summed = lax.psum(local_mix.astype(jnp.bfloat16), "comp").astype(jnp.float32)
        own_part = lax.dynamic_slice_in_dim(summed, comp_index * channel_width, channel_width, 0)
        blended = (own_part * own_beam[:, None, None, :]).astype(jnp.bfloat16)
        coeffs = jnp.einsum(
            "fkml,mlr->fkmr", blended, legendre_slot, preferred_element_type=jnp.float32
        ).astype(jnp.bfloat16)
        arrived = lax.all_to_all(coeffs, "blk", split_axis=3, concat_axis=2, tiled=True)
        sky_map = jnp.einsum("fkmq,qkmp->fqp", arrived, stored, preferred_element_type=jnp.float32)
        weighted = (weights[:, :, None] * inv_noise * sky_map).astype(jnp.bfloat16)
        projected = jnp.einsum(
            "fqp,qkmp->fkmq", weighted, stored, preferred_element_type=jnp.float32
        ).astype(jnp.bfloat16)
        returned = lax.all_to_all(projected, "blk", split_axis=2, concat_axis=3, tiled=True)
        harmonic = jnp.einsum(
            "fkms,mls->fkml", returned, legendre_slot, preferred_element_type=jnp.float32
        )
        everyone = lax.all_gather(
            harmonic.astype(jnp.bfloat16), ("comp", "lat"), axis=0, tiled=True
        ).astype(harmonic.dtype)
        stacked = everyone.reshape(
            (lax.axis_size("comp"), lax.axis_size("lat"), channel_width) + harmonic.shape[1:]
        )
        summed_bands = jnp.sum(stacked, axis=1).reshape((-1,) + harmonic.shape[1:])
        backward = jnp.einsum(
            "fc,fkml->ckml",
            mixing,
            summed_bands * beam[:, None, None, :],
            precision=HIGHEST_PRECISION,
        )
        applied = prior[:, None, None, :] * direction + backward
        totals = lax.psum(
            (
                jnp.sum(direction * applied),
                jnp.sum(residual * applied),
                jnp.sum(applied * applied),
                jnp.sum(residual * residual),
            ),
            ("blk", "comp"),
        )
        curvature, cross_term, square, norm_now = totals
        step_size = norm_now / curvature
        solution = solution + step_size * direction
        residual = residual - step_size * applied
        norm_next = norm_now - 2.0 * step_size * cross_term + step_size * step_size * square
        direction = residual + norm_next / norm_now * direction
    return (solution, residual)


def solution(mesh):
    in_specs = (
        P(("groups", "comp"), None, "blk", None),
        P("blk", None, "lat"),
        P(),
        P(None, "comp"),
        P("comp", None),
        P("comp", ("blk", "lat"), None),
        P("comp", ("blk", "lat")),
        P("lat"),
        P("lat"),
        P(),
    )
    out_specs = (P(("groups", "comp"), None, "blk", None), P(("groups", "comp"), None, "blk", None))
    return jax.shard_map(local, mesh=mesh, in_specs=in_specs, out_specs=out_specs, check_vma=False)
```

profile of v0, /device:TPU:0, one launch (start us, length us, event | category | flops | bytes accessed | tf_op | source)
XLA Modules:
  0.0 247.4 jit_solution(14166799779424596444)
XLA Ops:
  7.2 0.0 all-reduce.7.cloned.1.call-start
  7.2 2.3 fusion.12
  9.6 0.0 all-reduce.7.cloned.1.call-update
  9.6 0.6 copy-done.10
  10.3 0.1 compare_select_fusion.1
  10.3 0.6 copy-done.1
  10.9 0.6 gather_fusion.1
  11.6 0.1 iota_compare_fusion
  11.7 0.6 copy-done.7
  12.3 0.1 broadcast_multiply_fusion
  12.5 0.6 gather_fusion
  13.1 0.3 copy-done.3
  13.4 22.6 %all-reduce.7.cloned.1.call-done = bf16[24,2,1,2048]{3,0,1,2:T(8,128)(2,1)} async-done(((bf16[24,2,1,2048]{3,0,1,2:T(8,128)(2,1)}), bf16[24,2,1,2048]{3,0,1,2:T(8,128)(2,1)}) %all-reduce.7.cloned.1.call-update) | async-done | bytes 196624 | tf_op jit(solution)/shard_map/psum | solution.py:40
  36.0 1.2 fusion.18
  37.2 0.6 copy.87
  37.8 4.6 %all-to-all-start = ((bf16[12,2,1,16]{0,1,2,3:T(2,128)(2,1)}), bf16[12,2,1,16]{0,1,2,3:T(2,128)(2,1)S(1)}, u32[]{:S(2)}, u32[]{:S(2)}) async-start(bf16[12,2,1,16]{0,1,2,3:T(2,128)(2,1)} %copy.87), calls=%async_computation | async-start | bytes 16384 | tf_op jit(solution)/shard_map/all_to_all | solution.py:46
  42.4 7.2 %select_convert_fusion.1 = (bf16[1,4,4,4096]{3,2,0,1:T(4,128)(2,1)S(1)}, bf16[1,4,4,4096]{3,2,0,1:T(4,128)(2,1)S(1)}) fusion(f32[4]{0:T(128)S(1)} %get-tuple-element.32, pred[4]{0:T(512)(128)(4,1)S(1)} %broadcast_compare_fusion, s32[4]{0:T(128)S(1)} %get-tuple-element.31, s32[4,4096]{1,0:T(4,128)S(1)} %broadcast_multiply_fusion, ...), kind=kLoop, calls=%fused_computation.88 | loop fusion | flops 983040 | bytes 344100 | tf_op jit(solution)/shard_map/convert.3
  49.7 1.0 fusion.19
  50.7 0.6 copy.90
  51.3 5.1 %all-to-all-start.1 = ((bf16[12,2,4,4]{0,1,3,2:T(2,128)(2,1)}), bf16[12,2,4,4]{0,1,3,2:T(2,128)(2,1)S(1)}, u32[]{:S(2)}, u32[]{:S(2)}) async-start(bf16[12,2,4,4]{0,1,3,2:T(2,128)(2,1)} %copy.90), calls=%async_computation.1 | async-start | bytes 16384 | tf_op jit(solution)/shard_map/all_to_all | solution.py:52
  56.4 1.4 multiply_reduce_fusion.8
  57.8 4.2 %all-to-all-done.1 = bf16[12,2,4,4]{0,1,3,2:T(2,128)(2,1)S(1)} async-done(((bf16[12,2,4,4]{0,1,3,2:T(2,128)(2,1)}), bf16[12,2,4,4]{0,1,3,2:T(2,128)(2,1)S(1)}, u32[]{:S(2)}, u32[]{:S(2)}) %all-to-all-start.1) | async-done | bytes 800 | tf_op jit(solution)/shard_map/all_to_all | solution.py:52
  62.0 0.2 fusion.15
  62.2 0.1 copy.93
  62.3 6.1 %all_gather.9 = bf16[48,2,1,2048]{3,1,2,0:T(2,128)(2,1)S(1)} all-gather(bf16[12,2,1,2048]{3,1,2,0:T(2,128)(2,1)S(1)} %copy.93), channel_id=1, replica_groups=mesh['groups'=2,'blk'=4,'comp'=2,'lat'=2] {'comp','lat'}, dimensions={0}, use_global_device_ids=true | all-gather | bytes 491520 | tf_op jit(solution)/shard_map/all_gather | solution.py:56
  68.5 0.4 convert_reduce_fusion.2
  69.0 0.2 bitcast_multiply_fusion.2
  69.2 0.6 copy-done.4
  69.9 1.5 multiply_reduce_fusion.5
  71.4 18.6 %all-reduce.2 = (f32[]{:T(128)}, f32[]{:T(128)}, f32[]{:T(128)}) all-reduce(f32[]{:T(128)} %multiply_reduce_fusion.8, f32[]{:T(128)} %get-tuple-element.15, f32[]{:T(128)} %get-tuple-element.14), channel_id=1, replica_groups=mesh['groups'=2,'blk'=4,'comp'=2,'lat'=2] {'blk','comp'}, use_global_device_ids=true, to_apply=%region_1.2 | all-reduce | flops 3 | bytes 24 | tf_op jit(solution)/shard_map/psum | solution.py:70
  93.8 0.3 multiply_add_fusion.2
  94.1 1.1 fusion.13
  95.2 0.0 all-reduce.9.cloned.1.call-update
  95.2 0.0 all-reduce.11.cloned.1.call-start
  95.3 20.3 %all-reduce.9.cloned.1.call-done = bf16[24,2,1,2048]{3,0,1,2:T(8,128)(2,1)} async-done(((bf16[24,2,1,2048]{3,0,1,2:T(8,128)(2,1)}), bf16[24,2,1,2048]{3,0,1,2:T(8,128)(2,1)}) %all-reduce.9.cloned.1.call-update) | async-done | bytes 196624 | tf_op jit(solution)/shard_map/psum | solution.py:40
  115.6 1.2 fusion.20
  116.8 10.0 %all_to_all.63 = bf16[12,2,1,16]{0,1,2,3:T(2,128)(2,1)S(1)} all-to-all(bf16[12,2,1,16]{0,1,2,3:T(2,128)(2,1)S(1)} %copy.100), channel_id=1, replica_groups=mesh['groups'=2,'blk'=4,'comp'=2,'lat'=2] {'blk'}, dimensions={3} | all-to-all | bytes 1536 | tf_op jit(solution)/shard_map/all_to_all | solution.py:46
  126.8 1.0 fusion.21
  127.9 7.9 %all_to_all.64 = bf16[12,2,4,4]{0,1,3,2:T(2,128)(2,1)S(1)} all-to-all(bf16[12,2,4,4]{0,1,3,2:T(2,128)(2,1)S(1)} %copy.103), channel_id=1, replica_groups=mesh['groups'=2,'blk'=4,'comp'=2,'lat'=2] {'blk'}, dimensions={2} | all-to-all | bytes 1536 | tf_op jit(solution)/shard_map/all_to_all | solution.py:52
  135.8 0.2 fusion.16
  136.0 0.1 copy.106
  136.2 6.3 %all_gather.10 = bf16[48,2,1,2048]{3,1,2,0:T(2,128)(2,1)S(1)} all-gather(bf16[12,2,1,2048]{3,1,2,0:T(2,128)(2,1)S(1)} %copy.106), channel_id=1, replica_groups=mesh['groups'=2,'blk'=4,'comp'=2,'lat'=2] {'comp','lat'}, dimensions={0}, use_global_device_ids=true | all-gather | bytes 491520 | tf_op jit(solution)/shard_map/all_gather | solution.py:56
  142.5 0.4 convert_reduce_fusion.1
  142.9 0.2 bitcast_multiply_fusion.1
  143.2 1.5 multiply_reduce_fusion.1
  144.6 18.7 %all-reduce.1 = (f32[]{:T(128)}, f32[]{:T(128)}, f32[]{:T(128)}, f32[]{:T(128)}) all-reduce(f32[]{:T(128)} %get-tuple-element.12, f32[]{:T(128)} %get-tuple-element.13, f32[]{:T(128)} %get-tuple-element.11, f32[]{:T(128)} %get-tuple-element.10), channel_id=1, replica_groups=mesh['groups'=2,'blk'=4,'comp'=2,'lat'=2] {'blk','comp'}, use_global_device_ids=true, to_apply=%region_7.8 | all-reduce | flops 4 | bytes 32 | tf_op jit(solution)/shard_map/psum | solution.py:70
  167.2 0.7 multiply_reduce_fusion.3
  168.0 1.1 fusion.14
  169.1 0.0 all-reduce.11.cloned.1.call-update
  169.2 20.4 %all-reduce.11.cloned.1.call-done = bf16[24,2,1,2048]{3,0,1,2:T(8,128)(2,1)} async-done(((bf16[24,2,1,2048]{3,0,1,2:T(8,128)(2,1)}), bf16[24,2,1,2048]{3,0,1,2:T(8,128)(2,1)}) %all-reduce.11.cloned.1.call-update) | async-done | bytes 196624 | tf_op jit(solution)/shard_map/psum | solution.py:40
  189.5 1.2 fusion.22
  190.8 10.0 %all_to_all.65 = bf16[12,2,1,16]{0,1,2,3:T(2,128)(2,1)S(1)} all-to-all(bf16[12,2,1,16]{0,1,2,3:T(2,128)(2,1)S(1)} %copy.109), channel_id=1, replica_groups=mesh['groups'=2,'blk'=4,'comp'=2,'lat'=2] {'blk'}, dimensions={3} | all-to-all | bytes 1536 | tf_op jit(solution)/shard_map/all_to_all | solution.py:46
  200.8 1.0 fusion.23
  201.8 7.9 %all_to_all.66 = bf16[12,2,4,4]{0,1,3,2:T(2,128)(2,1)S(1)} all-to-all(bf16[12,2,4,4]{0,1,3,2:T(2,128)(2,1)S(1)} %copy.112), channel_id=1, replica_groups=mesh['groups'=2,'blk'=4,'comp'=2,'lat'=2] {'blk'}, dimensions={2} | all-to-all | bytes 1536 | tf_op jit(solution)/shard_map/all_to_all | solution.py:52
  209.7 0.2 fusion.17
  210.0 0.1 copy.115
  210.1 6.1 %all_gather.11 = bf16[48,2,1,2048]{3,1,2,0:T(2,128)(2,1)S(1)} all-gather(bf16[12,2,1,2048]{3,1,2,0:T(2,128)(2,1)S(1)} %copy.115), channel_id=1, replica_groups=mesh['groups'=2,'blk'=4,'comp'=2,'lat'=2] {'comp','lat'}, dimensions={0}, use_global_device_ids=true | all-gather | bytes 491520 | tf_op jit(solution)/shard_map/all_gather | solution.py:56
  216.2 0.4 convert_reduce_fusion
  216.7 0.3 bitcast_multiply_fusion
  216.9 1.3 multiply_reduce_fusion
  218.3 18.6 %all-reduce = (f32[]{:T(128)}, f32[]{:T(128)}) all-reduce(f32[]{:T(128)} %get-tuple-element.25, f32[]{:T(128)} %get-tuple-element.35), channel_id=1, replica_groups=mesh['groups'=2,'blk'=4,'comp'=2,'lat'=2] {'blk','comp'}, use_global_device_ids=true, to_apply=%region_15.16 | all-reduce | flops 2 | bytes 16 | tf_op jit(solution)/shard_map/psum | solution.py:70
  238.2 0.3 multiply_subtract_fusion
  238.5 1.2 copy.119
  239.7 1.1 copy.118
  (32 shorter events, 0.2 us)
Async XLA Ops:
  7.2 5.3 %copy-start = (bf16[1,2048,16]{1,2,0:T(8,128)(2,1)S(1)}, bf16[1,2048,16]{1,2,0:T(8,128)(2,1)}, u32[]{:S(2)}) copy-start(bf16[1,2048,16]{1,2,0:T(8,128)(2,1)} %param.11) | copy-start | bytes 196612
  7.2 28.8 %all-reduce.7.cloned.1.call-start = ((), (), s32[]{:S(2)}) async-start(), calls=%async_computation.6 | async-start | bytes 393216 | tf_op jit(solution)/shard_map/psum | solution.py:40
  9.6 0.7 copy-start.10
  10.3 0.7 copy-start.1
  11.7 0.7 copy-start.7
  12.4 0.9 copy-start.3
  13.4 36.3 %copy-start.8 = (f32[12,4,4096]{2,1,0:T(4,128)S(1)}, f32[12,4,4096]{2,1,0:T(4,128)}, u32[]{:S(2)}) copy-start(f32[12,4,4096]{2,1,0:T(4,128)} %param.15) | copy-start | bytes 2359300
  37.8 11.8 %all-to-all-start = ((bf16[12,2,1,16]{0,1,2,3:T(2,128)(2,1)}), bf16[12,2,1,16]{0,1,2,3:T(2,128)(2,1)S(1)}, u32[]{:S(2)}, u32[]{:S(2)}) async-start(bf16[12,2,1,16]{0,1,2,3:T(2,128)(2,1)} %copy.87), calls=%async_computation | async-start | bytes 16384 | tf_op jit(solution)/shard_map/all_to_all | solution.py:46
  42.4 7.2 %copy-start.6 = (s32[12,4]{0,1:T(4,128)S(1)}, s32[12,4]{0,1:T(4,128)}, u32[]{:S(2)}) copy-start(s32[12,4]{0,1:T(4,128)} %param.16) | copy-start | bytes 580
  49.7 6.8 %copy-start.2 = (f32[24,2,1,2048]{3,2,1,0:T(1,128)S(1)}, f32[24,2,1,2048]{3,2,1,0:T(1,128)}, u32[]{:S(2)}) copy-start(f32[24,2,1,2048]{3,2,1,0:T(1,128)} %param.10) | copy-start | bytes 1179652
  51.3 10.7 %all-to-all-start.1 = ((bf16[12,2,4,4]{0,1,3,2:T(2,128)(2,1)}), bf16[12,2,4,4]{0,1,3,2:T(2,128)(2,1)S(1)}, u32[]{:S(2)}, u32[]{:S(2)}) async-start(bf16[12,2,4,4]{0,1,3,2:T(2,128)(2,1)} %copy.90), calls=%async_computation.1 | async-start | bytes 16384 | tf_op jit(solution)/shard_map/all_to_all | solution.py:52
  56.4 59.2 %all-reduce.9.cloned.1.call-start = ((), (), s32[]{:S(2)}) async-start(), calls=%async_computation.7 | async-start | bytes 393216 | tf_op jit(solution)/shard_map/psum | solution.py:40
  68.9 0.9 copy-start.4
  69.0 0.9 copy-start.5
  95.2 94.3 %all-reduce.11.cloned.1.call-start = ((), (), s32[]{:S(2)}) async-start(), calls=%async_computation.8 | async-start | bytes 393216 | tf_op jit(solution)/shard_map/psum | solution.py:40
  168.0 32.8 %copy-start.9 = (f32[12,4,4096]{2,1,0:T(4,128)S(1)}, f32[12,4,4096]{2,1,0:T(4,128)}, u32[]{:S(2)}) copy-start(f32[12,4,4096]{2,1,0:T(4,128)} %param.15) | copy-start | bytes 2359300
Sparse Core Ops, SparseCore 0:
  10.8 25.1 all-reduce.6
  95.4 20.2 all-reduce.8
  169.3 20.2 all-reduce.10
where the time goes:
time: 248 us; the launch traced here: 247 us
  blocking collectives  110 us (44%)
  waiting for transfers between devices  67.6 us (27%)
  between operations  23.1 us (9%)
  matrix products  16.3 us (7%)
  other arithmetic  12.3 us (5%)
  starting transfers between devices  9.77 us (4%)
  local copies, waits for them, and re-layouts  8.04 us (3%)
    psum x3, waiting for transfers between devices, local(): lax.psum(local_mix.astype(jnp.bfloat16), 'comp').astype(jnp.float32)  63.3 us
    psum x3, blocking collectives, local(): lax.psum((jnp.sum(direction * applied), jnp.sum(residual * applied), jnp....  55.9 us
    all_to_all x2, blocking collectives, local(): lax.all_to_all(coeffs, 'blk', split_axis=3, concat_axis=2, tiled=True)  20 us
    all_gather x3, blocking collectives, local(): lax.all_gather(harmonic.astype(jnp.bfloat16), ('comp', 'lat'), axis=0, ti...  18.6 us
    all_to_all x2, blocking collectives, local(): lax.all_to_all(projected, 'blk', split_axis=2, concat_axis=3, tiled=True)  15.9 us
    another operation x1, other arithmetic  7.19 us
    unnamed x24, local copies, waits for them, and re-layouts  5.18 us
    all_to_all x1, starting transfers between devices, local(): lax.all_to_all(projected, 'blk', split_axis=2, concat_axis=3, tiled=True)  5.09 us
  transfers between devices with their start and end apart: 5, of which 4 were waited for; matrix products, arithmetic and copies ran while one was open for 4% of the time, Pallas kernels for 0%

commit v1 on v0

--- a/solution.py
+++ b/solution.py
@@ -37,7 +37,9 @@
     direction = rhs
     for iteration in range(ITERS):
         local_mix = jnp.einsum("fc,ckml->fkml", mixing, direction, precision=HIGHEST_PRECISION)
-        summed = lax.psum(local_mix.astype(jnp.bfloat16), "comp").astype(jnp.float32)
+        summed = jnp.sum(lax.all_gather(local_mix.astype(jnp.bfloat16), "comp"), axis=0).astype(
+            jnp.float32
+        )
         own_part = lax.dynamic_slice_in_dim(summed, comp_index * channel_width, channel_width, 0)
         blended = (own_part * own_beam[:, None, None, :]).astype(jnp.bfloat16)
         coeffs = jnp.einsum(

time: 248 us -> 186 us (0.75)
  waiting for transfers between devices: 67.6 us -> 4.18 us
  blocking collectives: 110 us -> 128 us
  between operations: 23.1 us -> 9.98 us
  matrix products: 16.3 us -> 12.6 us
    psum x3 -> x0, waiting for transfers between devices: 63.3 us -> none  [local(): lax.psum(local_mix.astype(jnp.bfloat16), 'comp').astype(jnp.float32)]
    all_gather x0 -> x3, blocking collectives: none -> 21.2 us  [local(): lax.all_gather(local_mix.astype(jnp.bfloat16), 'comp')]
    all_to_all x2, blocking collectives: 20 us -> 15.9 us  [local(): lax.all_to_all(coeffs, 'blk', split_axis=3, concat_axis=2, tiled=True)]
    dot_general x3, matrix products: 3.57 us -> 0.83 us  [local(): jnp.einsum('fkml,mlr->fkmr', blended, legendre_slot, preferred_element_ty...]
    unnamed x24 -> x22, local copies, waits for them, and re-layouts: 5.18 us -> 4.64 us
  transfers between devices with their start and end apart: 5 -> 2, of which waited for: 4 -> 1; matrix products, arithmetic and copies ran while one was open for 4% -> 5% of each run, Pallas kernels for 0% -> 0%
where the time goes in v1:
time: 186 us
  blocking collectives  128 us (69%)
  other arithmetic  12.7 us (7%)
  matrix products  12.6 us (7%)
  starting transfers between devices  10.2 us (5%)
  between operations  9.98 us (5%)
  local copies, waits for them, and re-layouts  7.5 us (4%)
  waiting for transfers between devices  4.18 us (2%)
    psum x3, blocking collectives, local(): lax.psum((jnp.sum(direction * applied), jnp.sum(residual * applied), jnp....  56.5 us
    all_gather x3, blocking collectives, local(): lax.all_gather(local_mix.astype(jnp.bfloat16), 'comp')  21.2 us
    all_gather x3, blocking collectives, local(): lax.all_gather(harmonic.astype(jnp.bfloat16), ('comp', 'lat'), axis=0, ti...  18.9 us
    all_to_all x2, blocking collectives, local(): lax.all_to_all(projected, 'blk', split_axis=2, concat_axis=3, tiled=True)  15.9 us
    all_to_all x2, blocking collectives, local(): lax.all_to_all(coeffs, 'blk', split_axis=3, concat_axis=2, tiled=True)  15.9 us
    another operation x1, other arithmetic  7.21 us
    all_to_all x1, starting transfers between devices, local(): lax.all_to_all(coeffs, 'blk', split_axis=3, concat_axis=2, tiled=True)  5.12 us
    all_to_all x1, starting transfers between devices, local(): lax.all_to_all(projected, 'blk', split_axis=2, concat_axis=3, tiled=True)  5.09 us
  transfers between devices with their start and end apart: 2, of which 1 were waited for; matrix products, arithmetic and copies ran while one was open for 5% of the time, Pallas kernels for 0%

profile of v1, /device:TPU:0, one launch (start us, length us, event | category | flops | bytes accessed | tf_op | source)
XLA Modules:
  0.0 185.6 jit_solution(16393596295415116612)
XLA Ops:
  0.6 0.0 copy-start
  0.7 0.7 copy-done.9
  1.4 0.0 copy-done.5
  1.4 1.6 convolution_convert_fusion.2
  3.0 8.5 %all-gather = bf16[48,2,2048]{2,0,1:T(8,128)(2,1)S(1)} all-gather(bf16[24,2,2048]{2,0,1:T(8,128)(2,1)S(1)} %convolution_convert_fusion.2), channel_id=2, replica_groups=mesh['groups'=2,'blk'=4,'comp'=2,'lat'=2] {'comp'}, dimensions={0}, use_global_device_ids=true | all-gather | bytes 589824 | tf_op jit(solution)/shard_map/all_gather | solution.py:40
  11.6 0.6 gather_fusion
  12.2 0.3 copy-done.3
  12.5 0.1 reduce.9
  12.6 0.3 fusion.17
  12.9 0.6 copy.87
  13.5 5.1 %all-to-all-start = ((bf16[12,2,1,16]{0,1,2,3:T(2,128)(2,1)}), bf16[12,2,1,16]{0,1,2,3:T(2,128)(2,1)S(1)}, u32[]{:S(2)}, u32[]{:S(2)}) async-start(bf16[12,2,1,16]{0,1,2,3:T(2,128)(2,1)} %copy.87), calls=%async_computation | async-start | bytes 16384 | tf_op jit(solution)/shard_map/all_to_all | solution.py:48
  18.7 0.1 compare_select_fusion.1
  18.8 0.6 gather_fusion.1
  19.4 0.1 iota_compare_fusion
  19.5 0.0 copy-start.7
  19.5 0.6 copy-done.7
  20.2 0.1 broadcast_multiply_fusion
  20.3 7.2 %select_convert_fusion.1 = (bf16[1,4,4,4096]{3,2,0,1:T(4,128)(2,1)S(1)}, bf16[1,4,4,4096]{3,2,0,1:T(4,128)(2,1)S(1)}) fusion(f32[4]{0:T(128)S(1)} %get-tuple-element.32, pred[4]{0:T(512)(128)(4,1)S(1)} %broadcast_compare_fusion, s32[4]{0:T(128)S(1)} %get-tuple-element.31, s32[4,4096]{1,0:T(4,128)S(1)} %broadcast_multiply_fusion, ...), kind=kLoop, calls=%fused_computation.90 | loop fusion | flops 983040 | bytes 344100 | tf_op jit(solution)/shard_map/convert.6
  27.5 1.0 fusion.18
  28.6 0.6 copy.90
  29.2 5.1 %all-to-all-start.1 = ((bf16[12,2,4,4]{0,1,3,2:T(2,128)(2,1)}), bf16[12,2,4,4]{0,1,3,2:T(2,128)(2,1)S(1)}, u32[]{:S(2)}, u32[]{:S(2)}) async-start(bf16[12,2,4,4]{0,1,3,2:T(2,128)(2,1)} %copy.90), calls=%async_computation.1 | async-start | bytes 16384 | tf_op jit(solution)/shard_map/all_to_all | solution.py:54
  34.3 1.4 multiply_reduce_fusion.8
  35.7 4.2 %all-to-all-done.1 = bf16[12,2,4,4]{0,1,3,2:T(2,128)(2,1)S(1)} async-done(((bf16[12,2,4,4]{0,1,3,2:T(2,128)(2,1)}), bf16[12,2,4,4]{0,1,3,2:T(2,128)(2,1)S(1)}, u32[]{:S(2)}, u32[]{:S(2)}) %all-to-all-start.1) | async-done | bytes 800 | tf_op jit(solution)/shard_map/all_to_all | solution.py:54
  39.9 0.2 fusion.14
  40.1 0.1 copy.93
  40.2 6.5 %all_gather.29 = bf16[48,2,1,2048]{3,1,2,0:T(2,128)(2,1)S(1)} all-gather(bf16[12,2,1,2048]{3,1,2,0:T(2,128)(2,1)S(1)} %copy.93), channel_id=1, replica_groups=mesh['groups'=2,'blk'=4,'comp'=2,'lat'=2] {'comp','lat'}, dimensions={0}, use_global_device_ids=true | all-gather | bytes 491520 | tf_op jit(solution)/shard_map/all_gather | solution.py:58
  46.7 0.5 convert_reduce_fusion.2
  47.1 0.3 bitcast_multiply_fusion.2
  47.4 0.6 copy-done.4
  48.1 1.5 multiply_reduce_fusion.5
  49.6 18.9 %all-reduce.2 = (f32[]{:T(128)}, f32[]{:T(128)}, f32[]{:T(128)}) all-reduce(f32[]{:T(128)} %multiply_reduce_fusion.8, f32[]{:T(128)} %get-tuple-element.15, f32[]{:T(128)} %get-tuple-element.14), channel_id=1, replica_groups=mesh['groups'=2,'blk'=4,'comp'=2,'lat'=2] {'blk','comp'}, use_global_device_ids=true, to_apply=%region_1.2 | all-reduce | flops 3 | bytes 24 | tf_op jit(solution)/shard_map/psum | solution.py:72
  72.3 0.3 multiply_add_fusion.2
  72.6 0.5 fusion.12
  73.1 6.3 %all-gather.1 = bf16[48,2,2048]{2,0,1:T(8,128)(2,1)S(1)} all-gather(bf16[24,2,2048]{2,0,1:T(8,128)(2,1)S(1)} %fusion.12), channel_id=3, replica_groups=mesh['groups'=2,'blk'=4,'comp'=2,'lat'=2] {'comp'}, dimensions={0}, use_global_device_ids=true | all-gather | bytes 589824 | tf_op jit(solution)/shard_map/all_gather | solution.py:40
  79.4 0.1 reduce.10
  79.5 0.3 fusion.19
  79.8 7.9 %all_to_all.63 = bf16[12,2,1,16]{0,1,2,3:T(2,128)(2,1)S(1)} all-to-all(bf16[12,2,1,16]{0,1,2,3:T(2,128)(2,1)S(1)} %copy.100), channel_id=1, replica_groups=mesh['groups'=2,'blk'=4,'comp'=2,'lat'=2] {'blk'}, dimensions={3} | all-to-all | bytes 1536 | tf_op jit(solution)/shard_map/all_to_all | solution.py:48
  87.7 1.0 fusion.20
  88.8 7.9 %all_to_all.64 = bf16[12,2,4,4]{0,1,3,2:T(2,128)(2,1)S(1)} all-to-all(bf16[12,2,4,4]{0,1,3,2:T(2,128)(2,1)S(1)} %copy.103), channel_id=1, replica_groups=mesh['groups'=2,'blk'=4,'comp'=2,'lat'=2] {'blk'}, dimensions={2} | all-to-all | bytes 1536 | tf_op jit(solution)/shard_map/all_to_all | solution.py:54
  96.7 0.2 fusion.15
  96.9 0.1 copy.106
  97.1 6.3 %all_gather.32 = bf16[48,2,1,2048]{3,1,2,0:T(2,128)(2,1)S(1)} all-gather(bf16[12,2,1,2048]{3,1,2,0:T(2,128)(2,1)S(1)} %copy.106), channel_id=1, replica_groups=mesh['groups'=2,'blk'=4,'comp'=2,'lat'=2] {'comp','lat'}, dimensions={0}, use_global_device_ids=true | all-gather | bytes 491520 | tf_op jit(solution)/shard_map/all_gather | solution.py:58
  103.4 0.5 convert_reduce_fusion.1
  103.8 0.3 bitcast_multiply_fusion.1
  104.1 1.4 multiply_reduce_fusion.1
  105.6 18.7 %all-reduce.1 = (f32[]{:T(128)}, f32[]{:T(128)}, f32[]{:T(128)}, f32[]{:T(128)}) all-reduce(f32[]{:T(128)} %get-tuple-element.12, f32[]{:T(128)} %get-tuple-element.13, f32[]{:T(128)} %get-tuple-element.11, f32[]{:T(128)} %get-tuple-element.10), channel_id=1, replica_groups=mesh['groups'=2,'blk'=4,'comp'=2,'lat'=2] {'blk','comp'}, use_global_device_ids=true, to_apply=%region_7.8 | all-reduce | flops 4 | bytes 32 | tf_op jit(solution)/shard_map/psum | solution.py:72
  128.2 0.7 multiply_reduce_fusion.3
  128.9 0.5 fusion.13
  129.4 6.3 %all-gather.2 = bf16[48,2,2048]{2,0,1:T(8,128)(2,1)S(1)} all-gather(bf16[24,2,2048]{2,0,1:T(8,128)(2,1)S(1)} %fusion.13), channel_id=4, replica_groups=mesh['groups'=2,'blk'=4,'comp'=2,'lat'=2] {'comp'}, dimensions={0}, use_global_device_ids=true | all-gather | bytes 589824 | tf_op jit(solution)/shard_map/all_gather | solution.py:40
  135.7 0.1 reduce.11
  135.8 0.3 fusion.21
  136.1 7.9 %all_to_all.65 = bf16[12,2,1,16]{0,1,2,3:T(2,128)(2,1)S(1)} all-to-all(bf16[12,2,1,16]{0,1,2,3:T(2,128)(2,1)S(1)} %copy.109), channel_id=1, replica_groups=mesh['groups'=2,'blk'=4,'comp'=2,'lat'=2] {'blk'}, dimensions={3} | all-to-all | bytes 1536 | tf_op jit(solution)/shard_map/all_to_all | solution.py:48
  144.0 2.2 %fusion.22 = bf16[12,2,4,4]{0,2,1,3:T(4,128)(2,1)S(1)} fusion(f32[12,4,4096]{2,1,0:T(4,128)} %param.15, f32[12,4]{0,1:T(4,128)S(1)} %convert_element_type.180, bf16[12,2,4,4]{0,1,3,2:T(2,128)(2,1)S(1)} %bitcast.224, bf16[1,4,4,4096]{3,2,0,1:T(4,128)(2,1)S(1)} %get-tuple-element.30, bf16[1,4,4,4096]{3,2,0,1:T(4,128)(2,1)S(1)} %get-tuple-element.29), kind=kOutput, calls=%fused_computation.42 | convolution fusion | flops 7930240 | bytes 1050304 | tf_op jit(solution)/shard_map/fqp,qkmp->fkmq/dot_general | solution.py:51
  146.2 7.9 %all_to_all.66 = bf16[12,2,4,4]{0,1,3,2:T(2,128)(2,1)S(1)} all-to-all(bf16[12,2,4,4]{0,1,3,2:T(2,128)(2,1)S(1)} %copy.112), channel_id=1, replica_groups=mesh['groups'=2,'blk'=4,'comp'=2,'lat'=2] {'blk'}, dimensions={2} | all-to-all | bytes 1536 | tf_op jit(solution)/shard_map/all_to_all | solution.py:54
  154.2 0.2 fusion.16
  154.4 0.1 copy.115
  154.5 6.1 %all_gather.35 = bf16[48,2,1,2048]{3,1,2,0:T(2,128)(2,1)S(1)} all-gather(bf16[12,2,1,2048]{3,1,2,0:T(2,128)(2,1)S(1)} %copy.115), channel_id=1, replica_groups=mesh['groups'=2,'blk'=4,'comp'=2,'lat'=2] {'comp','lat'}, dimensions={0}, use_global_device_ids=true | all-gather | bytes 491520 | tf_op jit(solution)/shard_map/all_gather | solution.py:58
  160.6 0.5 convert_reduce_fusion
  161.1 0.3 bitcast_multiply_fusion
  161.4 1.3 multiply_reduce_fusion
  162.7 18.9 %all-reduce = (f32[]{:T(128)}, f32[]{:T(128)}) all-reduce(f32[]{:T(128)} %get-tuple-element.25, f32[]{:T(128)} %get-tuple-element.35), channel_id=1, replica_groups=mesh['groups'=2,'blk'=4,'comp'=2,'lat'=2] {'blk','comp'}, use_global_device_ids=true, to_apply=%region_15.16 | all-reduce | flops 2 | bytes 16 | tf_op jit(solution)/shard_map/psum | solution.py:72
  183.0 0.4 multiply_subtract_fusion
  183.3 1.2 copy.119
  184.5 1.1 copy.118
  (27 shorter events, 0.2 us)
Async XLA Ops:
  0.6 10.9 %copy-start = (bf16[1,2048,16]{1,2,0:T(8,128)(2,1)S(1)}, bf16[1,2048,16]{1,2,0:T(8,128)(2,1)}, u32[]{:S(2)}) copy-start(bf16[1,2048,16]{1,2,0:T(8,128)(2,1)} %param.11) | copy-start | bytes 196612
  0.6 0.7 copy-start.5
  0.7 0.7 copy-start.9
  11.6 0.9 copy-start.3
  12.6 6.1 %copy-start.1 = (s32[16]{0:T(128)S(1)}, s32[16]{0:T(128)}, u32[]{:S(2)}) copy-start(s32[16]{0:T(128)} %param.17) | copy-start | bytes 196
  12.6 14.9 %copy-start.8 = (f32[12,4,4096]{2,1,0:T(4,128)S(1)}, f32[12,4,4096]{2,1,0:T(4,128)}, u32[]{:S(2)}) copy-start(f32[12,4,4096]{2,1,0:T(4,128)} %param.15) | copy-start | bytes 2359300
  13.5 14.0 %all-to-all-start = ((bf16[12,2,1,16]{0,1,2,3:T(2,128)(2,1)}), bf16[12,2,1,16]{0,1,2,3:T(2,128)(2,1)S(1)}, u32[]{:S(2)}, u32[]{:S(2)}) async-start(bf16[12,2,1,16]{0,1,2,3:T(2,128)(2,1)} %copy.87), calls=%async_computation | async-start | bytes 16384 | tf_op jit(solution)/shard_map/all_to_all | solution.py:48
  19.5 0.7 copy-start.7
  20.2 7.2 %copy-start.6 = (s32[12,4]{0,1:T(4,128)S(1)}, s32[12,4]{0,1:T(4,128)}, u32[]{:S(2)}) copy-start(s32[12,4]{0,1:T(4,128)} %param.16) | copy-start | bytes 580
  27.5 6.8 %copy-start.2 = (f32[24,2,1,2048]{3,2,1,0:T(1,128)S(1)}, f32[24,2,1,2048]{3,2,1,0:T(1,128)}, u32[]{:S(2)}) copy-start(f32[24,2,1,2048]{3,2,1,0:T(1,128)} %param.10) | copy-start | bytes 1179652
  29.2 10.7 %all-to-all-start.1 = ((bf16[12,2,4,4]{0,1,3,2:T(2,128)(2,1)}), bf16[12,2,4,4]{0,1,3,2:T(2,128)(2,1)S(1)}, u32[]{:S(2)}, u32[]{:S(2)}) async-start(bf16[12,2,4,4]{0,1,3,2:T(2,128)(2,1)} %copy.90), calls=%async_computation.1 | async-start | bytes 16384 | tf_op jit(solution)/shard_map/all_to_all | solution.py:54
  47.1 0.9 copy-start.4
